TPU v7x, 128 devices: a whole 4x4x4 slice. The times are simulated.
128 devices in a mesh: ctx: 32 (over x, y, core), row: 4 (over z).
Axes of the slice: x: 4, y: 4, z: 4, core: 2. Of those that a mesh axis runs over, the one named last changes fastest.
Arguments:
- latent_cache: bfloat16 [131072, 576], P(('ctx', 'row')), may hold values from -8 to 8
- index_keys: bfloat16 [131072, 128], P('ctx'), may hold values from -6 to 6
- query_latent: bfloat16 [512, 128, 576], P(('row', 'ctx')), may hold values from -100 to 99
- index_query: bfloat16 [512, 64, 128], P(('row', 'ctx')), may hold values from -0.5 to 0.5
- index_gates: bfloat16 [512, 64], P(('row', 'ctx')), may hold values from -0.75 to 0.75
- selected: int32 [512, 2048], P(('row', 'ctx')), may hold values from 0 to 131071, as said below
Outputs:
- attended: bfloat16 [512, 128, 512], P(('row', 'ctx'))
- index_scores: float32 [512, 131072], P('row', 'ctx')
Inputs may be any that keep to these rules, and one draw needn't show every extreme that they name: `selected`: each row names 2048 different tokens. Among the tokens of one index of ctx (s * 4096 <= t < (s + 1) * 4096) a row names at most 256, and exactly 256 in one such range; a row names at most one token in each aligned run of 16 tokens.
All inputs are finite; a program needn't handle non-finite values.
Results may differ from a plain program's by a relative error of at most 0.0045.
Values may be sent and summed in bfloat16 or wider, within the bound.
A program may use at most 256 MiB of HBM per device.

v0:
```python
import jax
import jax.numpy as jnp
from jax import lax
from jax.sharding import PartitionSpec as P

LATENT = 512
SCORE_DIM = 192
SEL_MOST = 256
TOK_DEV = 4096


def index_block(iquery, gates, index_keys):
    count = iquery.shape[0]
    groups = count // 8
    heads = iquery.shape[1]
    query_blocks = iquery.reshape(groups, 8 * heads, iquery.shape[2])
    gate_blocks = gates.astype(jnp.float32).reshape(groups, 8, heads)

    def one_block(pair):
        block, gate = pair
        logits = jnp.einsum("qd,td->qt", block, index_keys, preferred_element_type=jnp.float32)
        logits = logits.reshape(8, heads, logits.shape[1])
        return jnp.sum(gate[:, :, None] * jnp.maximum(logits, 0.0), axis=1)

    result = lax.map(one_block, (query_blocks, gate_blocks))
    return result.reshape(count, result.shape[2])


def slot_table(place, value, slots):

    def one_row(pair):
        where_to, what = pair
        hit = where_to[:, None] == jnp.arange(slots, dtype=jnp.int32)[None, :]
        return jnp.max(jnp.where(hit, what[:, None], -1), axis=0)

    return lax.map(one_row, (place, value))


def pick_rows(source, table, spacing):
    blocks = source.reshape(source.shape[0] // spacing, spacing, source.shape[1])
    offset = table % spacing
    onehot = (
        (offset[:, :, None] == jnp.arange(spacing, dtype=jnp.int32)[None, None, :])
        & (table >= 0)[:, :, None]
    ).astype(jnp.bfloat16)
    rows_out = jnp.einsum("gsj,sjd->gsd", onehot, blocks, preferred_element_type=jnp.float32)
    return rows_out.astype(jnp.bfloat16)


def weigh(queries, keys, valid):
    scores = jnp.einsum(
        "ghd,gsd->ghs", queries, keys, preferred_element_type=jnp.float32
    ) * SCORE_DIM ** (-0.5)
    return jnp.where(valid[:, None, :], scores, -1e30)


def combine(masked, peak, keys, valid):
    weights = jnp.where(valid[:, None, :], jnp.exp(masked - peak[:, :, None]), 0.0).astype(
        jnp.bfloat16
    )
    totals = jnp.sum(weights.astype(jnp.float32), axis=2)
    sums = jnp.einsum(
        "ghs,gsd->ghd", weights, keys[:, :, :LATENT], preferred_element_type=jnp.float32
    )
    return (sums, totals)


def body(latent_cache, index_keys, query_latent, index_query, index_gates, selected):
    spacing = TOK_DEV // SEL_MOST
    slab = lax.all_gather(latent_cache, "row", axis=0, tiled=True)
    queries, iquery, gates = (
        lax.all_gather(query_latent, "ctx", axis=0, tiled=True),
        lax.all_gather(index_query, "ctx", axis=0, tiled=True),
        lax.all_gather(index_gates, "ctx", axis=0, tiled=True),
    )
    picks = lax.all_gather(selected, "ctx", axis=0, tiled=True)
    index_scores = index_block(iquery, gates, index_keys)
    local = picks - lax.axis_index("ctx") * TOK_DEV
    mine = (local >= 0) & (local < TOK_DEV)
    place = jnp.where(mine, local // spacing, SEL_MOST)
    table = slot_table(place, local, SEL_MOST)
    valid = table >= 0
    keys = pick_rows(slab, table, spacing)
    masked = weigh(queries, keys, valid)
    peak = lax.pmax(jnp.max(masked, axis=2), "ctx")
    sums, totals = combine(masked, peak, keys, valid)
    summed, total = (
        lax.psum_scatter(sums, "ctx", scatter_dimension=0, tiled=True),
        lax.psum_scatter(totals, "ctx", scatter_dimension=0, tiled=True),
    )
    attended = (summed / total[:, :, None]).astype(jnp.bfloat16)
    return (attended, index_scores)


def solution(mesh):
    return jax.shard_map(
        body,
        mesh=mesh,
        in_specs=(
            P(("ctx", "row"), None),
            P("ctx", None),
            P(("row", "ctx"), None, None),
            P(("row", "ctx"), None, None),
            P(("row", "ctx"), None),
            P(("row", "ctx"), None),
        ),
        out_specs=(P(("row", "ctx"), None, None), P("row", "ctx")),
        check_vma=False,
    )
```

profile of v0, /device:TPU:1, one launch (start us, length us, event | category | flops | bytes accessed | tf_op | source)
XLA Modules:
  0.0 751.0 jit_solution(6434805967596199768)
XLA Ops:
  9.4 46.8 %all-gather.13.cloned.1.call-done = s32[32,4,2048]{2,1,0:T(4,128)} async-done(((s32[1,4,2048]{2,1,0:T(4,128)}), s32[32,4,2048]{2,1,0:T(4,128)}) %all-gather.13.cloned.1.call-update) | async-done | bytes 1048592 | tf_op jit(solution)/shard_map/all_gather | solution.py:76
  56.2 1.3 broadcast_subtract_fusion
  58.6 166.7 %while.22 = (s32[]{:T(128)}, s32[128,256]{1,0:T(8,128)S(1)}, s32[128,2048]{1,0:T(8,128)S(1)}, s32[128,2048]{1,0:T(8,128)S(1)}) while((s32[]{:T(128)}, s32[128,256]{1,0:T(8,128)S(1)}, s32[128,2048]{1,0:T(8,128)S(1)}, s32[128,2048]{1,0:T(8,128)S(1)}) %tuple.46), condition=%wide.region_2.3_spmd.clone, body=%wide.region_0.2_spmd.sunk.clone | while | flops 1572610 | bytes 52293 | solution.py:36
  225.7 7.6 %copy.22 = bf16[4096,576]{1,0:T(8,128)(2,1)} copy(bf16[4096,576]{0,1:T(8,128)(2,1)} %all-gather.7.cloned.1.call-done) | data formatting | bytes 9437184 | tf_op jit(solution)/shard_map/all_gather | solution.py:70
  233.4 18.0 %convert_bitcast_fusion = bf16[128,256,576]{0,2,1:T(8,128)(2,1)} fusion(bf16[256,16,576]{2,1,0:T(8,128)(2,1)} %bitcast.69, s32[128,256]{0,1:T(8,128)S(1)} %copy.20, pred[128,256]{0,1:T(8,128)(4,1)S(1)} %copy.21), kind=kOutput, calls=%fused_computation.9 | convolution fusion | flops 623902720 | bytes 42631168 | tf_op jit(solution)/shard_map/gsj,sjd->gsd/dot_general | solution.py:46
  251.4 51.8 %copy.23 = bf16[128,256,576]{1,2,0:T(8,128)(2,1)} copy(bf16[128,256,576]{0,2,1:T(8,128)(2,1)} %convert_bitcast_fusion) | data formatting | bytes 75497472 | tf_op jit(solution)/shard_map/convert_element_type | solution.py:47
  303.2 30.3 %bitcast_reduce_fusion = (f32[128,128]{1,0:T(8,128)}, f32[128,256,128]{2,1,0:T(8,128)}) fusion(pred[128,256]{1,0:T(8,128)(4,1)S(1)} %broadcast_compare_fusion, bf16[128,256,576]{1,2,0:T(8,128)(2,1)} %copy.23, bf16[128,128,576]{1,2,0:T(8,128)(2,1)} %all-gather.9.cloned.1.call-done), kind=kOutput, calls=%fused_computation.11 | convolution fusion | flops 4844404736 | bytes 73498624 | tf_op jit(solution)/shard_map/ghd,gsd->ghs/dot_general | solution.py:51
  334.2 23.0 %slice.4 = bf16[128,256,512]{0,2,1:T(8,128)(2,1)} slice(bf16[128,256,576]{0,2,1:T(8,128)(2,1)} %convert_bitcast_fusion), slice={[0:128], [0:256], [0:512]} | slice | bytes 67108864 | tf_op jit(solution)/shard_map/slice | solution.py:63
  357.2 44.9 %copy.25 = bf16[128,256,512]{2,1,0:T(8,128)(2,1)} copy(bf16[128,256,512]{0,2,1:T(8,128)(2,1)} %slice.4) | data formatting | bytes 67108864 | tf_op jit(solution)/shard_map/slice | solution.py:63
  402.0 28.0 %all-reduce.4.cloned.1.call-done = f32[128,128]{1,0:T(8,128)} async-done(((f32[128,128]{1,0:T(8,128)}), f32[128,128]{1,0:T(8,128)}) %all-reduce.4.cloned.1.call-update) | async-done | bytes 65552 | tf_op jit(solution)/shard_map/pmax | solution.py:85
  430.0 14.2 %convert_reduce_fusion = f32[128,128]{1,0:T(8,128)} fusion(f32[128,128]{1,0:T(8,128)} %all-reduce.4.cloned.1.call-done, f32[128,256,128]{2,1,0:T(8,128)} %get-tuple-element.74, pred[128,256]{1,0:T(8,128)(4,1)S(1)} %broadcast_compare_fusion), kind=kLoop, calls=%fused_computation.15 | loop fusion | flops 29343744 | bytes 16941056 | tf_op jit(solution)/shard_map/reduce_sum | solution.py:61
  444.5 32.7 %fusion.12 = f32[128,128,512]{2,1,0:T(8,128)} fusion(bf16[128,256,512]{2,1,0:T(8,128)(2,1)} %copy.25, f32[128,256,128]{2,1,0:T(8,128)} %get-tuple-element.74, f32[128,128]{1,0:T(8,128)S(1)} %copy-done, pred[128,256]{1,0:T(8,128)(4,1)S(1)} %broadcast_compare_fusion), kind=kOutput, calls=%fused_computation.38 | convolution fusion | flops 4315938816 | bytes 83984384 | tf_op jit(solution)/shard_map/ghs,gsd->ghd/dot_general | solution.py:62
  479.1 23.1 %all-gather.1 = bf16[32,4,64]{2,1,0:T(4,128)(2,1)S(1)} all-gather(bf16[1,4,64]{2,1,0:T(4,128)(2,1)S(1)} %bitcast.79), channel_id=1, replica_groups=mesh['ctx'=32,'row'=4] {'ctx'}, dimensions={0}, use_global_device_ids=true | all-gather | bytes 16896 | tf_op jit(solution)/shard_map/all_gather | solution.py:74
  502.2 46.3 %while.23 = (s32[]{:T(128)}, f32[16,8,4096]{2,1,0:T(8,128)}, f32[16,8,64]{2,1,0:T(8,128)S(1)}, bf16[16,512,128]{2,1,0:T(8,128)(2,1)}, bf16[4096,128]{1,0:T(8,128)(2,1)S(1)}) while((s32[]{:T(128)}, f32[16,8,4096]{2,1,0:T(8,128)}, f32[16,8,64]{2,1,0:T(8,128)S(1)}, bf16[16,512,128]{2,1,0:T(8,128)(2,1)}, ...), condition=%wide.region_10.11_spmd.clone, body=%wide.region_8.10_spmd.sunk.clone | while | flops 543129600 | bytes 1841233 | solution.py:25
  506.1 1.3 multiply_reduce_fusion.3
  509.0 1.3 multiply_reduce_fusion.3
  520.6 1.3 multiply_reduce_fusion.3
  526.3 1.3 multiply_reduce_fusion.3
  532.1 1.3 multiply_reduce_fusion.3
  537.9 1.3 multiply_reduce_fusion.3
  540.8 1.3 multiply_reduce_fusion.3
  548.6 26.0 %all-reduce.6.cloned.1.call-done = f32[128,128]{1,0:T(8,128)} async-done(((f32[128,128]{1,0:T(8,128)}), f32[128,128]{1,0:T(8,128)}) %all-reduce.6.cloned.1.call-update) | async-done | bytes 65552
  575.2 166.7 %reduce-scatter.2.cloned.1.call-done = f32[4,128,512]{2,1,0:T(8,128)} async-done(((f32[128,128,512]{2,1,0:T(8,128)}), f32[4,128,512]{2,1,0:T(8,128)}) %reduce-scatter.2.cloned.1.call-update) | async-done | bytes 1048592 | tf_op jit(solution)/shard_map/reduce_scatter | solution.py:88
  742.0 2.2 divide_convert_fusion
  (477 shorter events, 206.3 us)
Async XLA Ops:
  7.2 49.1 %all-gather.13.cloned.1.call-start = ((), (), s32[]{:S(2)}) async-start(), calls=%async_computation.6 | async-start | bytes 1081344 | tf_op jit(solution)/shard_map/all_gather | solution.py:76
  7.9 217.8 %all-gather.7.cloned.1.call-start = ((), (), s32[]{:S(2)}) async-start(), calls=%async_computation.1 | async-start | bytes 5898240 | tf_op jit(solution)/shard_map/all_gather | solution.py:70
  8.6 294.6 %all-gather.9.cloned.1.call-start = ((), (), s32[]{:S(2)}) async-start(), calls=%async_computation.2 | async-start | bytes 19464192 | tf_op jit(solution)/shard_map/all_gather | solution.py:72
  9.4 420.6 %all-reduce.4.cloned.1.call-start = ((), (), s32[]{:S(2)}) async-start(), calls=%async_computation.3 | async-start | bytes 131072 | tf_op jit(solution)/shard_map/pmax | solution.py:85
  333.5 168.7 %all-gather.11.cloned.1.call-start = ((), (), s32[]{:S(2)}) async-start(), calls=%async_computation.5 | async-start | bytes 2162688 | tf_op jit(solution)/shard_map/all_gather | solution.py:73
  334.1 240.4 %all-reduce.6.cloned.1.call-start = ((), (), s32[]{:S(2)}) async-start(), calls=%async_computation.7 | async-start | bytes 131072
  430.0 14.5 %copy-start = (f32[128,128]{1,0:T(8,128)S(1)}, f32[128,128]{1,0:T(8,128)}, u32[]{:S(2)}) copy-start(f32[128,128]{1,0:T(8,128)} %all-reduce.4.cloned.1.call-done) | copy-start | bytes 196612
  444.3 297.7 %reduce-scatter.2.cloned.1.call-start = ((), (), s32[]{:S(2)}) async-start(), calls=%async_computation.4 | async-start | bytes 34603008 | tf_op jit(solution)/shard_map/reduce_scatter | solution.py:88
  477.2 0.7 copy-start.3
  477.2 1.9 copy-start.1
  477.2 25.1 %copy-start.2 = (bf16[4096,128]{1,0:T(8,128)(2,1)S(1)}, bf16[4096,128]{1,0:T(8,128)(2,1)}, u32[]{:S(2)}) copy-start(bf16[4096,128]{1,0:T(8,128)(2,1)} %param.11) | copy-start | bytes 3145732
Sparse Core Ops, SparseCore 0:
  10.2 45.9 all-gather.12
  57.9 51.6 all-gather.6
  111.9 78.0 all-gather.8
  333.7 96.3 all-reduce.3
  432.1 42.4 all-gather.10
  478.3 96.2 all-reduce.5
  578.4 163.4 reduce-scatter.1
where the time goes:
time: 754 us; the launch traced here: 751 us
  waiting for transfers between devices  270 us (36%)
  other arithmetic  173 us (23%)
  local copies, waits for them, and re-layouts  163 us (22%)
  matrix products  101 us (13%)
  blocking collectives  23.1 us (3%)
  between operations  14.9 us (2%)
    reduce_scatter x1, waiting for transfers between devices, body(): lax.psum_scatter(sums, 'ctx', scatter_dimension=0, tiled=True)  167 us
    reduce_max x128, other arithmetic, one_row(): return jnp.max(jnp.where(hit, what[:, None], -1), axis=0)  155 us
    slice x2, local copies, waits for them, and re-layouts, combine(): keys[:, :, :LATENT]  67.9 us
    convert_element_type x1, local copies, waits for them, and re-layouts, pick_rows(): return rows_out.astype(jnp.bfloat16)  51.8 us
    all_gather x1, waiting for transfers between devices, body(): picks = lax.all_gather(selected, 'ctx', axis=0, tiled=True)  46.8 us
    dot_general x1, matrix products, combine(): jnp.einsum('ghs,gsd->ghd', weights, keys[:, :, :LATENT], preferred_elemen...  32.7 us
    dot_general x1, matrix products, weigh(): jnp.einsum('ghd,gsd->ghs', queries, keys, preferred_element_type=jnp.floa...  30.3 us
    unnamed x8, waiting for transfers between devices  28.6 us
  transfers between devices with their start and end apart: 7, of which 4 were waited for; matrix products, arithmetic and copies ran while one was open for 54% of the time, Pallas kernels for 0%

commit v1 on v0

--- a/solution.py
+++ b/solution.py
@@ -73,7 +73,9 @@
         lax.all_gather(index_query, "ctx", axis=0, tiled=True),
         lax.all_gather(index_gates, "ctx", axis=0, tiled=True),
     )
-    picks = lax.all_gather(selected, "ctx", axis=0, tiled=True)
+    picks = jnp.concatenate(
+        lax.all_to_all(jnp.stack([selected] * lax.axis_size("ctx")), "ctx", 0, 0), axis=0
+    )
     index_scores = index_block(iquery, gates, index_keys)
     local = picks - lax.axis_index("ctx") * TOK_DEV
     mine = (local >= 0) & (local < TOK_DEV)

time: 754 us -> 731 us (0.969)
  waiting for transfers between devices: 270 us -> 240 us
  starting transfers between devices: 0.45 us -> 9 us
    all_gather x1 -> x0, waiting for transfers between devices: 46.8 us -> none  [body(): picks = lax.all_gather(selected, 'ctx', axis=0, tiled=True)]
    all_to_all x0 -> x1, waiting for transfers between devices: none -> 16.1 us  [body(): lax.all_to_all(jnp.stack([selected] * lax.axis_size('ctx')), 'ctx', 0, 0)]
    all_to_all x0 -> x1, starting transfers between devices: none -> 8.58 us  [body(): lax.all_to_all(jnp.stack([selected] * lax.axis_size('ctx')), 'ctx', 0, 0)]
    unnamed x8 -> x7, waiting for transfers between devices: 28.6 us -> 27.9 us
  transfers between devices with their start and end apart: 7 -> 7, of which waited for: 4 -> 4; matrix products, arithmetic and copies ran while one was open for 54% -> 55% of each run, Pallas kernels for 0% -> 0%
where the time goes in v1:
time: 731 us; the launch traced here: 728 us
  waiting for transfers between devices  240 us (33%)
  other arithmetic  172 us (24%)
  local copies, waits for them, and re-layouts  163 us (22%)
  matrix products  101 us (14%)
  blocking collectives  23.1 us (3%)
  between operations  15 us (2%)
  starting transfers between devices  9 us (1%)
    reduce_scatter x1, waiting for transfers between devices, body(): lax.psum_scatter(sums, 'ctx', scatter_dimension=0, tiled=True)  166 us
    reduce_max x128, other arithmetic, one_row(): return jnp.max(jnp.where(hit, what[:, None], -1), axis=0)  155 us
    slice x2, local copies, waits for them, and re-layouts, combine(): keys[:, :, :LATENT]  65.6 us
    convert_element_type x1, local copies, waits for them, and re-layouts, pick_rows(): return rows_out.astype(jnp.bfloat16)  52 us
    dot_general x1, matrix products, combine(): jnp.einsum('ghs,gsd->ghd', weights, keys[:, :, :LATENT], preferred_elemen...  32.7 us
    dot_general x1, matrix products, weigh(): jnp.einsum('ghd,gsd->ghs', queries, keys, preferred_element_type=jnp.floa...  30.3 us
    pmax x1, waiting for transfers between devices, body(): peak = lax.pmax(jnp.max(masked, axis=2), 'ctx')  29.6 us
    unnamed x7, waiting for transfers between devices  27.9 us
  transfers between devices with their start and end apart: 7, of which 4 were waited for; matrix products, arithmetic and copies ran while one was open for 55% of the time, Pallas kernels for 0%

profile of v1, /device:TPU:1, one launch (start us, length us, event | category | flops | bytes accessed | tf_op | source)
XLA Modules:
  0.0 728.2 jit_solution(13690168536128693705)
XLA Ops:
  7.9 2.0 stack.2
  9.9 8.6 %all-to-all-start = ((s32[32,4,2048]{2,1,0:T(4,128)}), s32[32,4,2048]{2,1,0:T(4,128)S(1)}, u32[]{:S(2)}, u32[]{:S(2)}) async-start(s32[32,4,2048]{2,1,0:T(4,128)} %stack.2), calls=%async_computation | async-start | bytes 2097152 | tf_op jit(solution)/shard_map/all_to_all | solution.py:77
  19.3 16.1 %all-to-all-done = s32[32,4,2048]{2,1,0:T(4,128)S(1)} async-done(((s32[32,4,2048]{2,1,0:T(4,128)}), s32[32,4,2048]{2,1,0:T(4,128)S(1)}, u32[]{:S(2)}, u32[]{:S(2)}) %all-to-all-start) | async-done | bytes 1048608 | tf_op jit(solution)/shard_map/all_to_all | solution.py:77
  36.5 166.7 %while.22 = (s32[]{:T(128)}, s32[128,256]{1,0:T(8,128)S(1)}, s32[128,2048]{1,0:T(8,128)S(1)}, s32[128,2048]{1,0:T(8,128)S(1)}) while((s32[]{:T(128)}, s32[128,256]{1,0:T(8,128)S(1)}, s32[128,2048]{1,0:T(8,128)S(1)}, s32[128,2048]{1,0:T(8,128)S(1)}) %tuple.46), condition=%wide.region_2.3_spmd.clone, body=%wide.region_0.2_spmd.sunk.clone | while | flops 1572610 | bytes 52293 | solution.py:36
  203.6 7.7 %copy.22 = bf16[4096,576]{1,0:T(8,128)(2,1)} copy(bf16[4096,576]{0,1:T(8,128)(2,1)} %all-gather.5.cloned.1.call-done) | data formatting | bytes 9437184 | tf_op jit(solution)/shard_map/all_gather | solution.py:70
  211.3 18.0 %convert_bitcast_fusion = bf16[128,256,576]{0,2,1:T(8,128)(2,1)} fusion(bf16[256,16,576]{2,1,0:T(8,128)(2,1)} %bitcast.68, s32[128,256]{0,1:T(8,128)S(1)} %copy.20, pred[128,256]{0,1:T(8,128)(4,1)S(1)} %copy.21), kind=kOutput, calls=%fused_computation.9 | convolution fusion | flops 623902720 | bytes 42631168 | tf_op jit(solution)/shard_map/gsj,sjd->gsd/dot_general | solution.py:46
  229.3 52.0 %copy.23 = bf16[128,256,576]{1,2,0:T(8,128)(2,1)} copy(bf16[128,256,576]{0,2,1:T(8,128)(2,1)} %convert_bitcast_fusion) | data formatting | bytes 75497472 | tf_op jit(solution)/shard_map/convert_element_type | solution.py:47
  281.2 30.3 %bitcast_reduce_fusion = (f32[128,128]{1,0:T(8,128)}, f32[128,256,128]{2,1,0:T(8,128)}) fusion(pred[128,256]{1,0:T(8,128)(4,1)S(1)} %broadcast_compare_fusion, bf16[128,256,576]{1,2,0:T(8,128)(2,1)} %copy.23, bf16[128,128,576]{1,2,0:T(8,128)(2,1)} %all-gather.7.cloned.1.call-done), kind=kOutput, calls=%fused_computation.11 | convolution fusion | flops 4844404736 | bytes 73498624 | tf_op jit(solution)/shard_map/ghd,gsd->ghs/dot_general | solution.py:51
  312.4 23.0 %slice.4 = bf16[128,256,512]{0,2,1:T(8,128)(2,1)} slice(bf16[128,256,576]{0,2,1:T(8,128)(2,1)} %convert_bitcast_fusion), slice={[0:128], [0:256], [0:512]} | slice | bytes 67108864 | tf_op jit(solution)/shard_map/slice | solution.py:63
  335.3 42.6 %copy.25 = bf16[128,256,512]{2,1,0:T(8,128)(2,1)} copy(bf16[128,256,512]{0,2,1:T(8,128)(2,1)} %slice.4) | data formatting | bytes 67108864 | tf_op jit(solution)/shard_map/slice | solution.py:63
  377.9 29.6 %all-reduce.4.cloned.1.call-done = f32[128,128]{1,0:T(8,128)} async-done(((f32[128,128]{1,0:T(8,128)}), f32[128,128]{1,0:T(8,128)}) %all-reduce.4.cloned.1.call-update) | async-done | bytes 65552 | tf_op jit(solution)/shard_map/pmax | solution.py:87
  407.6 14.2 %convert_reduce_fusion = f32[128,128]{1,0:T(8,128)} fusion(f32[128,128]{1,0:T(8,128)} %all-reduce.4.cloned.1.call-done, f32[128,256,128]{2,1,0:T(8,128)} %get-tuple-element.74, pred[128,256]{1,0:T(8,128)(4,1)S(1)} %broadcast_compare_fusion), kind=kLoop, calls=%fused_computation.15 | loop fusion | flops 29343744 | bytes 16941056 | tf_op jit(solution)/shard_map/reduce_sum | solution.py:61
  421.9 32.7 %fusion.12 = f32[128,128,512]{2,1,0:T(8,128)} fusion(bf16[128,256,512]{2,1,0:T(8,128)(2,1)} %copy.25, f32[128,256,128]{2,1,0:T(8,128)} %get-tuple-element.74, f32[128,128]{1,0:T(8,128)S(1)} %copy-done, pred[128,256]{1,0:T(8,128)(4,1)S(1)} %broadcast_compare_fusion), kind=kOutput, calls=%fused_computation.38 | convolution fusion | flops 4315938816 | bytes 83984384 | tf_op jit(solution)/shard_map/ghs,gsd->ghd/dot_general | solution.py:62
  456.5 23.1 %all-gather = bf16[32,4,64]{2,1,0:T(4,128)(2,1)S(1)} all-gather(bf16[1,4,64]{2,1,0:T(4,128)(2,1)S(1)} %bitcast.77), channel_id=1, replica_groups=mesh['ctx'=32,'row'=4] {'ctx'}, dimensions={0}, use_global_device_ids=true | all-gather | bytes 16896 | tf_op jit(solution)/shard_map/all_gather | solution.py:74
  479.7 46.3 %while.23 = (s32[]{:T(128)}, f32[16,8,4096]{2,1,0:T(8,128)}, f32[16,8,64]{2,1,0:T(8,128)S(1)}, bf16[16,512,128]{2,1,0:T(8,128)(2,1)}, bf16[4096,128]{1,0:T(8,128)(2,1)S(1)}) while((s32[]{:T(128)}, f32[16,8,4096]{2,1,0:T(8,128)}, f32[16,8,64]{2,1,0:T(8,128)S(1)}, bf16[16,512,128]{2,1,0:T(8,128)(2,1)}, ...), condition=%wide.region_10.11_spmd.clone, body=%wide.region_8.10_spmd.sunk.clone | while | flops 543129600 | bytes 1841233 | solution.py:25
  483.6 1.3 multiply_reduce_fusion.3
  486.5 1.3 multiply_reduce_fusion.3
  489.4 1.3 multiply_reduce_fusion.3
  503.8 1.3 multiply_reduce_fusion.3
  506.7 1.3 multiply_reduce_fusion.3
  518.3 1.3 multiply_reduce_fusion.3
  526.1 26.0 %all-reduce.6.cloned.1.call-done = f32[128,128]{1,0:T(8,128)} async-done(((f32[128,128]{1,0:T(8,128)}), f32[128,128]{1,0:T(8,128)}) %all-reduce.6.cloned.1.call-update) | async-done | bytes 65552
  552.7 166.5 %reduce-scatter.2.cloned.1.call-done = f32[4,128,512]{2,1,0:T(8,128)} async-done(((f32[128,128,512]{2,1,0:T(8,128)}), f32[4,128,512]{2,1,0:T(8,128)}) %reduce-scatter.2.cloned.1.call-update) | async-done | bytes 1048592 | tf_op jit(solution)/shard_map/reduce_scatter | solution.py:90
  719.2 2.2 divide_convert_fusion
  (477 shorter events, 206.9 us)
Async XLA Ops:
  7.2 196.5 %all-gather.5.cloned.1.call-start = ((), (), s32[]{:S(2)}) async-start(), calls=%async_computation.2 | async-start | bytes 5898240 | tf_op jit(solution)/shard_map/all_gather | solution.py:70
  9.9 25.5 %all-to-all-start = ((s32[32,4,2048]{2,1,0:T(4,128)}), s32[32,4,2048]{2,1,0:T(4,128)S(1)}, u32[]{:S(2)}, u32[]{:S(2)}) async-start(s32[32,4,2048]{2,1,0:T(4,128)} %stack.2), calls=%async_computation | async-start | bytes 2097152 | tf_op jit(solution)/shard_map/all_to_all | solution.py:77
  18.4 262.8 %all-gather.7.cloned.1.call-start = ((), (), s32[]{:S(2)}) async-start(), calls=%async_computation.3 | async-start | bytes 19464192 | tf_op jit(solution)/shard_map/all_gather | solution.py:72
  19.2 388.3 %all-reduce.4.cloned.1.call-start = ((), (), s32[]{:S(2)}) async-start(), calls=%async_computation.4 | async-start | bytes 131072 | tf_op jit(solution)/shard_map/pmax | solution.py:87
  311.5 168.2 %all-gather.9.cloned.1.call-start = ((), (), s32[]{:S(2)}) async-start(), calls=%async_computation.6 | async-start | bytes 2162688 | tf_op jit(solution)/shard_map/all_gather | solution.py:73
  312.1 239.9 %all-reduce.6.cloned.1.call-start = ((), (), s32[]{:S(2)}) async-start(), calls=%async_computation.7 | async-start | bytes 131072
  407.5 14.3 %copy-start = (f32[128,128]{1,0:T(8,128)S(1)}, f32[128,128]{1,0:T(8,128)}, u32[]{:S(2)}) copy-start(f32[128,128]{1,0:T(8,128)} %all-reduce.4.cloned.1.call-done) | copy-start | bytes 196612
  421.8 297.4 %reduce-scatter.2.cloned.1.call-start = ((), (), s32[]{:S(2)}) async-start(), calls=%async_computation.5 | async-start | bytes 34603008 | tf_op jit(solution)/shard_map/reduce_scatter | solution.py:90
  454.5 0.7 copy-start.3
  454.5 2.0 copy-start.1
  454.5 25.2 %copy-start.2 = (bf16[4096,128]{1,0:T(8,128)(2,1)S(1)}, bf16[4096,128]{1,0:T(8,128)(2,1)}, u32[]{:S(2)}) copy-start(bf16[4096,128]{1,0:T(8,128)(2,1)} %param.11) | copy-start | bytes 3145732
Sparse Core Ops, SparseCore 0:
  9.6 55.8 all-gather.4
  67.7 78.0 all-gather.6
  311.7 95.8 all-reduce.3
  409.7 42.4 all-gather.8
  455.8 96.1 all-reduce.5
  555.8 163.3 reduce-scatter.1
